TPU v7x, 256 devices: a whole 4x4x8 slice. The times are simulated.
256 devices in a mesh: dp: 32 (over x_lo, z, core), tensor: 8 (over y, x_hi).
Axes of the slice: x: 4 (x_hi: 2, x_lo: 2; x = x_hi * 2 + x_lo), y: 4, z: 8, core: 2. Of those that a mesh axis runs over, the one named last changes fastest.
Arguments:
- tokens: bfloat16 [6144, 2048], P(('dp', 'tensor')), may hold values from -6 to 6
- grad_hidden: bfloat16 [6144, 5504], P('dp', 'tensor'), may hold values from -0.078125 to 0.078125
- width_in: bfloat16 [2048, 1024], P(None, 'tensor'), may hold values from -0.125 to 0.125
- gate_small: bfloat16 [1024, 2752], P(None, 'tensor'), may hold values from -0.1875 to 0.1875
- up_small: bfloat16 [1024, 2752], P(None, 'tensor'), may hold values from -0.1875 to 0.1875
- width_hidden: bfloat16 [5504, 2752], P('tensor'), may hold values from -0.109375 to 0.109375
Outputs:
- grad_width_in: float32 [2048, 1024], P('dp', 'tensor')
- grad_gate_small: float32 [1024, 2752], P('dp', 'tensor')
- grad_up_small: float32 [1024, 2752], P('dp', 'tensor')
- grad_width_hidden: float32 [5504, 2752], P('tensor', 'dp')
All inputs are finite; a program needn't handle non-finite values.
Results may differ from a plain program's by a relative error of at most 0.0085.
Values may be sent and summed in bfloat16 or wider, within the bound.
No kernel may reach another device: no remote copies, remote signals or barrier semaphores. Data moves between devices by JAX's collectives and lax.ppermute only.
A program may use at most 64 MiB of HBM per device.

v0:
```python
import jax
import jax.numpy as jnp
from jax import lax
from jax.sharding import PartitionSpec as P


def contract_rows(left, right):
    return lax.dot_general(
        left, right, (((0,), (0,)), ((), ())), preferred_element_type=jnp.float32
    )


def contract_cols(left, right):
    return lax.dot_general(
        left, right, (((1,), (1,)), ((), ())), preferred_element_type=jnp.float32
    )


def on_device(tokens, grad_hidden, width_in, gate_small, up_small, width_hidden):
    all_tokens = lax.all_gather(tokens, "tensor", axis=0, tiled=True)
    narrow_part = jnp.dot(all_tokens, width_in, preferred_element_type=jnp.float32).astype(
        jnp.bfloat16
    )
    narrow = lax.all_gather(narrow_part, "tensor", axis=1, tiled=True)
    gate_part = jnp.dot(narrow, gate_small, preferred_element_type=jnp.float32).astype(jnp.bfloat16)
    up_part = jnp.dot(narrow, up_small, preferred_element_type=jnp.float32).astype(jnp.bfloat16)
    gate_low, up_low = (
        lax.all_gather(gate_part, "tensor", axis=1, tiled=True),
        lax.all_gather(up_part, "tensor", axis=1, tiled=True),
    )
    gate_big = contract_cols(gate_low, width_hidden)
    up_big = contract_cols(up_low, width_hidden)
    upstream = grad_hidden.astype(jnp.float32)
    sig = jax.nn.sigmoid(gate_big)
    d_gate = (upstream * up_big * sig * (1.0 + gate_big * (1.0 - sig))).astype(jnp.bfloat16)
    d_up = (upstream * gate_big * sig).astype(jnp.bfloat16)
    hidden_term = contract_rows(gate_low, d_gate) + contract_rows(up_low, d_up)
    hidden_owned = lax.psum_scatter(hidden_term, "dp", scatter_dimension=0, tiled=True)
    gate_back = jnp.dot(d_gate, width_hidden, preferred_element_type=jnp.float32)
    up_back = jnp.dot(d_up, width_hidden, preferred_element_type=jnp.float32)
    gate_back_own, up_back_own = (
        lax.psum_scatter(gate_back, "tensor", scatter_dimension=1, tiled=True),
        lax.psum_scatter(up_back, "tensor", scatter_dimension=1, tiled=True),
    )
    d_gate_low = gate_back_own.astype(jnp.bfloat16)
    d_up_low = up_back_own.astype(jnp.bfloat16)
    gate_term = contract_rows(narrow, d_gate_low)
    up_term = contract_rows(narrow, d_up_low)
    grad_gate_small, grad_up_small = (
        lax.psum_scatter(gate_term, "dp", scatter_dimension=0, tiled=True),
        lax.psum_scatter(up_term, "dp", scatter_dimension=0, tiled=True),
    )
    narrow_back = contract_cols(d_gate_low, gate_small) + contract_cols(d_up_low, up_small)
    d_narrow = lax.psum_scatter(narrow_back, "tensor", scatter_dimension=1, tiled=True).astype(
        jnp.bfloat16
    )
    input_term = contract_rows(all_tokens, d_narrow)
    grad_width_in = lax.psum_scatter(input_term, "dp", scatter_dimension=0, tiled=True)
    return (grad_width_in, grad_gate_small, grad_up_small, hidden_owned.T)


def solution(mesh):
    return jax.shard_map(
        on_device,
        mesh=mesh,
        in_specs=(
            P(("dp", "tensor"), None),
            P("dp", "tensor"),
            P(None, "tensor"),
            P(None, "tensor"),
            P(None, "tensor"),
            P("tensor", None),
        ),
        out_specs=(P("dp", "tensor"), P("dp", "tensor"), P("dp", "tensor"), P("tensor", "dp")),
        check_vma=False,
    )
```

profile of v0, /device:TPU:8, one launch (start us, length us, event | category | flops | bytes accessed | tf_op | source)
XLA Modules:
  0.0 815.3 jit_solution(11428229200431129447)
XLA Ops:
  7.2 36.5 %all_gather.12 = bf16[192,2048]{1,0:T(8,128)(2,1)S(1)} all-gather(bf16[24,2048]{1,0:T(8,128)(2,1)} %param.6), channel_id=1, replica_groups=mesh['dp'=32,'tensor'=8] {'tensor'}, dimensions={0}, use_global_device_ids=true | all-gather | bytes 884736 | tf_op jit(solution)/shard_map/all_gather | solution.py:20
  43.7 1.4 convolution_convert_fusion.2
  45.1 33.1 %all_gather.13 = bf16[192,1024]{1,0:T(8,128)(2,1)S(1)} all-gather(bf16[192,128]{1,0:T(8,128)(2,1)S(1)} %convolution_convert_fusion.2), channel_id=1, replica_groups=mesh['dp'=32,'tensor'=8] {'tensor'}, dimensions={1}, use_global_device_ids=true | all-gather | bytes 442368 | tf_op jit(solution)/shard_map/all_gather | solution.py:24
  78.3 1.1 fusion.4
  80.6 52.1 %all-gather.5.cloned.1.call-done = bf16[8,344,192]{1,2,0:T(8,128)(2,1)} async-done(((bf16[1,344,192]{1,2,0:T(8,128)(2,1)}), bf16[8,344,192]{1,2,0:T(8,128)(2,1)}) %all-gather.5.cloned.1.call-update) | async-done | bytes 1056784 | tf_op jit(solution)/shard_map/all_gather | solution.py:29
  132.8 3.0 copy.14
  135.7 2.1 reshape.9
  137.8 48.5 %all-gather.7.cloned.1.call-done = bf16[8,344,192]{1,2,0:T(8,128)(2,1)} async-done(((bf16[1,344,192]{1,2,0:T(8,128)(2,1)}), bf16[8,344,192]{1,2,0:T(8,128)(2,1)}) %all-gather.7.cloned.1.call-update) | async-done | bytes 1056784 | tf_op jit(solution)/shard_map/all_gather | solution.py:28
  186.3 3.0 copy.15
  189.3 2.9 reshape.11
  192.1 3.9 fusion.18
  196.1 1.4 fusion.3
  197.5 3.4 convolution_bitcast_fusion.1
  200.9 5.6 convolution_bitcast_fusion
  206.6 76.9 %reduce-scatter.21.cloned.1.call-done = f32[344,192]{1,0:T(8,128)} async-done(((f32[2752,192]{1,0:T(8,128)}), f32[344,192]{1,0:T(8,128)}) %reduce-scatter.21.cloned.1.call-update) | async-done | bytes 264208
  283.5 1.1 copy.18
  284.6 1.3 fusion.22
  285.9 84.2 %reduce-scatter.23.cloned.1.call-done = f32[344,192]{1,0:T(8,128)} async-done(((f32[2752,192]{1,0:T(8,128)}), f32[344,192]{1,0:T(8,128)}) %reduce-scatter.23.cloned.1.call-update) | async-done | bytes 264208
  370.2 1.1 copy.20
  371.3 2.6 convolution_add_fusion.1
  374.0 1.7 fusion.21
  375.8 1.6 fusion.20
  377.7 2.6 fusion.19
  380.3 4.7 convolution_add_fusion
  385.0 65.2 %reduce-scatter.15.cloned.1.call-done = f32[192,128]{1,0:T(8,128)} async-done(((f32[192,1024]{1,0:T(8,128)}), f32[192,128]{1,0:T(8,128)}) %reduce-scatter.15.cloned.1.call-update) | async-done | bytes 98320 | tf_op jit(solution)/shard_map/reduce_scatter | solution.py:54
  450.3 1.2 convolution_bitcast_fusion.2
  451.5 1.3 copy.21
  452.9 83.5 %fusion = f32[88,688]{1,0:T(8,128)S(1)} fusion(f32[2752,688]{1,0:T(8,128)} %convolution_add_fusion), kind=kCustom, calls=%all-reduce-scatter | all-reduce-scatter fusion | flops 1937409 | bytes 7816704
  536.4 1.3 collective-permute-start
  540.0 32.8 %reduce-scatter.17.cloned.1.call-done = f32[32,344]{1,0:T(8,128)} async-done(((f32[1024,344]{1,0:T(8,128)}), f32[32,344]{1,0:T(8,128)}) %reduce-scatter.17.cloned.1.call-update) | async-done | bytes 44048 | tf_op jit(solution)/shard_map/reduce_scatter | solution.py:50
  572.8 118.3 %reduce-scatter.19.cloned.1.call-done = f32[32,344]{1,0:T(8,128)} async-done(((f32[1024,344]{1,0:T(8,128)}), f32[32,344]{1,0:T(8,128)}) %reduce-scatter.19.cloned.1.call-update) | async-done | bytes 44048 | tf_op jit(solution)/shard_map/reduce_scatter | solution.py:51
  691.1 117.3 %reduce-scatter.25.cloned.1.call-done = f32[64,128]{1,0:T(8,128)} async-done(((f32[2048,128]{1,0:T(8,128)}), f32[64,128]{1,0:T(8,128)}) %reduce-scatter.25.cloned.1.call-update) | async-done | bytes 32784
  (38 shorter events, 3.4 us)
Async XLA Ops:
  7.2 72.3 %copy-start = (bf16[1024,344]{0,1:T(8,128)(2,1)S(1)}, bf16[1024,344]{0,1:T(8,128)(2,1)}, u32[]{:S(2)}) copy-start(bf16[1024,344]{0,1:T(8,128)(2,1)} %param.9) | copy-start | bytes 2113540
  7.2 71.1 %copy-start.2 = (bf16[1024,344]{0,1:T(8,128)(2,1)S(1)}, bf16[1024,344]{0,1:T(8,128)(2,1)}, u32[]{:S(2)}) copy-start(bf16[1024,344]{0,1:T(8,128)(2,1)} %param.10) | copy-start | bytes 2113540
  7.2 125.6 %all-gather.5.cloned.1.call-start = ((), (), s32[]{:S(2)}) async-start(), calls=%async_computation.9 | async-start | bytes 1327104 | tf_op jit(solution)/shard_map/all_gather | solution.py:29
  79.4 106.9 %all-gather.7.cloned.1.call-start = ((), (), s32[]{:S(2)}) async-start(), calls=%async_computation.10 | async-start | bytes 1327104 | tf_op jit(solution)/shard_map/all_gather | solution.py:28
  80.6 202.9 %reduce-scatter.21.cloned.1.call-start = ((), (), s32[]{:S(2)}) async-start(), calls=%async_computation.11 | async-start | bytes 3170304
  192.1 3.9 copy-start.1
  192.1 3.9 copy-start.5
  196.1 1.4 copy-start.3
  200.8 169.3 %reduce-scatter.23.cloned.1.call-start = ((), (), s32[]{:S(2)}) async-start(), calls=%async_computation.12 | async-start | bytes 3170304
  206.5 243.7 %reduce-scatter.15.cloned.1.call-start = ((), (), s32[]{:S(2)}) async-start(), calls=%async_computation.6 | async-start | bytes 884736 | tf_op jit(solution)/shard_map/reduce_scatter | solution.py:54
  373.9 198.8 %reduce-scatter.17.cloned.1.call-start = ((), (), s32[]{:S(2)}) async-start(), calls=%async_computation.7 | async-start | bytes 1622016 | tf_op jit(solution)/shard_map/reduce_scatter | solution.py:50
  375.7 315.4 %reduce-scatter.19.cloned.1.call-start = ((), (), s32[]{:S(2)}) async-start(), calls=%async_computation.8 | async-start | bytes 1622016 | tf_op jit(solution)/shard_map/reduce_scatter | solution.py:51
  377.4 2.9 copy-start.6
  377.4 431.0 %reduce-scatter.25.cloned.1.call-start = ((), (), s32[]{:S(2)}) async-start(), calls=%async_computation.13 | async-start | bytes 1081344
  377.6 2.7 copy-start.4
  452.9 84.9 %copy-start.7 = (u32[256]{0:T(256)S(1)}, u32[256]{0:T(256)}, u32[]{:S(2)}) copy-start(u32[256]{0:T(256)} %constant.5) | copy-start | bytes 3076
  536.4 2.6 collective-permute-start
Sparse Core Ops, SparseCore 0:
  79.5 53.1 all-gather.4
  135.3 50.8 all-gather.6
  201.0 82.5 reduce-scatter.20
  287.5 82.6 reduce-scatter.22
  374.1 76.1 reduce-scatter.14
  453.2 119.5 reduce-scatter.16
  575.9 115.2 reduce-scatter.18
  694.2 114.1 reduce-scatter.24
where the time goes:
time: 816 us; the launch traced here: 815 us
  waiting for transfers between devices  596 us (73%)
  blocking collectives  153 us (19%)
  matrix products  33.6 us (4%)
  local copies, waits for them, and re-layouts  16.1 us (2%)
  between operations  15 us (2%)
    unnamed x12, waiting for transfers between devices  279 us
    reduce_scatter x1, waiting for transfers between devices, on_device(): lax.psum_scatter(up_term, 'dp', scatter_dimension=0, tiled=True)  118 us
    unnamed x1, blocking collectives  83.5 us
    reduce_scatter x1, waiting for transfers between devices, on_device(): lax.psum_scatter(narrow_back, 'tensor', scatter_dimension=1, tiled=True)  65.2 us
    all_gather x1, waiting for transfers between devices, on_device(): lax.all_gather(up_part, 'tensor', axis=1, tiled=True)  52.1 us
    all_gather x1, waiting for transfers between devices, on_device(): lax.all_gather(gate_part, 'tensor', axis=1, tiled=True)  48.5 us
    all_gather x1, blocking collectives, on_device(): all_tokens = lax.all_gather(tokens, 'tensor', axis=0, tiled=True)  36.5 us
    all_gather x1, blocking collectives, on_device(): narrow = lax.all_gather(narrow_part, 'tensor', axis=1, tiled=True)  33.1 us
  transfers between devices with their start and end apart: 9, of which 8 were waited for; matrix products, arithmetic and copies ran while one was open for 14% of the time, Pallas kernels for 0%

commit v1 on v0

--- a/solution.py
+++ b/solution.py
@@ -26,7 +26,9 @@
     up_part = jnp.dot(narrow, up_small, preferred_element_type=jnp.float32).astype(jnp.bfloat16)
     gate_low, up_low = (
         lax.all_gather(gate_part, "tensor", axis=1, tiled=True),
-        lax.all_gather(up_part, "tensor", axis=1, tiled=True),
+        jnp.concatenate(
+            lax.all_to_all(jnp.stack([up_part] * lax.axis_size("tensor")), "tensor", 0, 0), axis=1
+        ),
     )
     gate_big = contract_cols(gate_low, width_hidden)
     up_big = contract_cols(up_low, width_hidden)

time: 816 us -> 762 us (0.934)
  waiting for transfers between devices: 596 us -> 526 us
  blocking collectives: 153 us -> 172 us
    all_gather x1 -> x0, waiting for transfers between devices: 52.1 us -> none  [on_device(): lax.all_gather(up_part, 'tensor', axis=1, tiled=True)]
    all_to_all x0 -> x1, blocking collectives: none -> 18.4 us  [on_device(): lax.all_to_all(jnp.stack([up_part] * lax.axis_size('tensor')), 'tensor',...]
    all_gather x1, waiting for transfers between devices: 48.5 us -> 30.9 us  [on_device(): lax.all_gather(gate_part, 'tensor', axis=1, tiled=True)]
    unnamed x12 -> x11, waiting for transfers between devices: 279 us -> 279 us
  transfers between devices with their start and end apart: 9 -> 8, of which waited for: 8 -> 7; matrix products, arithmetic and copies ran while one was open for 14% -> 15% of each run, Pallas kernels for 0% -> 0%
where the time goes in v1:
time: 762 us
  waiting for transfers between devices  526 us (69%)
  blocking collectives  172 us (23%)
  matrix products  32.9 us (4%)
  local copies, waits for them, and re-layouts  15 us (2%)
  between operations  15 us (2%)
    unnamed x11, waiting for transfers between devices  279 us
    reduce_scatter x1, waiting for transfers between devices, on_device(): lax.psum_scatter(up_term, 'dp', scatter_dimension=0, tiled=True)  118 us
    unnamed x1, blocking collectives  83.5 us
    reduce_scatter x1, waiting for transfers between devices, on_device(): lax.psum_scatter(narrow_back, 'tensor', scatter_dimension=1, tiled=True)  65.2 us
    all_gather x1, blocking collectives, on_device(): all_tokens = lax.all_gather(tokens, 'tensor', axis=0, tiled=True)  36.5 us
    all_gather x1, blocking collectives, on_device(): narrow = lax.all_gather(narrow_part, 'tensor', axis=1, tiled=True)  33.2 us
    reduce_scatter x1, waiting for transfers between devices, on_device(): lax.psum_scatter(gate_term, 'dp', scatter_dimension=0, tiled=True)  32.7 us
    all_gather x1, waiting for transfers between devices, on_device(): lax.all_gather(gate_part, 'tensor', axis=1, tiled=True)  30.9 us
  transfers between devices with their start and end apart: 8, of which 7 were waited for; matrix products, arithmetic and copies ran while one was open for 15% of the time, Pallas kernels for 0%

profile of v1, /device:TPU:8, one launch (start us, length us, event | category | flops | bytes accessed | tf_op | source)
XLA Modules:
  0.0 762.0 jit_solution(13947187883937684502)
XLA Ops:
  7.2 36.5 %all_gather.9 = bf16[192,2048]{1,0:T(8,128)(2,1)S(1)} all-gather(bf16[24,2048]{1,0:T(8,128)(2,1)} %param.6), channel_id=1, replica_groups=mesh['dp'=32,'tensor'=8] {'tensor'}, dimensions={0}, use_global_device_ids=true | all-gather | bytes 884736 | tf_op jit(solution)/shard_map/all_gather | solution.py:20
  43.7 1.4 convolution_convert_fusion.2
  45.1 33.2 %all_gather.10 = bf16[192,1024]{1,0:T(8,128)(2,1)S(1)} all-gather(bf16[192,128]{1,0:T(8,128)(2,1)S(1)} %convolution_convert_fusion.2), channel_id=1, replica_groups=mesh['dp'=32,'tensor'=8] {'tensor'}, dimensions={1}, use_global_device_ids=true | all-gather | bytes 442368 | tf_op jit(solution)/shard_map/all_gather | solution.py:24
  78.4 1.1 fusion.4
  80.1 18.4 %all_to_all.5 = bf16[8,192,344]{2,1,0:T(8,128)(2,1)S(1)} all-to-all(bf16[8,192,344]{2,1,0:T(8,128)(2,1)S(1)} %stack.2), channel_id=1, replica_groups=mesh['dp'=32,'tensor'=8] {'tensor'}, dimensions={0} | all-to-all | bytes 2113536 | tf_op jit(solution)/shard_map/all_to_all | solution.py:30
  98.5 1.7 copy.13
  100.2 2.1 reshape.17
  102.3 30.9 %all-gather.3.cloned.1.call-done = bf16[8,344,192]{1,2,0:T(8,128)(2,1)} async-done(((bf16[1,344,192]{1,2,0:T(8,128)(2,1)}), bf16[8,344,192]{1,2,0:T(8,128)(2,1)}) %all-gather.3.cloned.1.call-update) | async-done | bytes 1056784 | tf_op jit(solution)/shard_map/all_gather | solution.py:28
  133.2 3.0 copy.14
  136.2 2.9 reshape.19
  139.0 3.9 fusion.17
  143.0 1.4 fusion.3
  144.3 3.4 convolution_bitcast_fusion.1
  147.8 5.6 convolution_bitcast_fusion
  153.5 77.0 %reduce-scatter.21.cloned.1.call-done = f32[344,192]{1,0:T(8,128)} async-done(((f32[2752,192]{1,0:T(8,128)}), f32[344,192]{1,0:T(8,128)}) %reduce-scatter.21.cloned.1.call-update) | async-done | bytes 264208
  230.4 1.1 copy.17
  231.6 1.3 fusion.21
  232.8 84.3 %reduce-scatter.23.cloned.1.call-done = f32[344,192]{1,0:T(8,128)} async-done(((f32[2752,192]{1,0:T(8,128)}), f32[344,192]{1,0:T(8,128)}) %reduce-scatter.23.cloned.1.call-update) | async-done | bytes 264208
  317.1 1.1 copy.19
  318.2 2.6 convolution_add_fusion.1
  320.9 1.7 fusion.20
  322.7 1.6 fusion.19
  324.6 2.6 fusion.18
  327.3 4.7 convolution_add_fusion
  331.9 65.2 %reduce-scatter.15.cloned.1.call-done = f32[192,128]{1,0:T(8,128)} async-done(((f32[192,1024]{1,0:T(8,128)}), f32[192,128]{1,0:T(8,128)}) %reduce-scatter.15.cloned.1.call-update) | async-done | bytes 98320 | tf_op jit(solution)/shard_map/reduce_scatter | solution.py:56
  397.2 1.2 convolution_bitcast_fusion.2
  398.4 1.3 copy.20
  399.8 83.5 %fusion = f32[88,688]{1,0:T(8,128)S(1)} fusion(f32[2752,688]{1,0:T(8,128)} %convolution_add_fusion), kind=kCustom, calls=%all-reduce-scatter | all-reduce-scatter fusion | flops 1937409 | bytes 7816704
  483.3 1.3 collective-permute-start
  486.9 32.7 %reduce-scatter.17.cloned.1.call-done = f32[32,344]{1,0:T(8,128)} async-done(((f32[1024,344]{1,0:T(8,128)}), f32[32,344]{1,0:T(8,128)}) %reduce-scatter.17.cloned.1.call-update) | async-done | bytes 44048 | tf_op jit(solution)/shard_map/reduce_scatter | solution.py:52
  519.6 117.8 %reduce-scatter.19.cloned.1.call-done = f32[32,344]{1,0:T(8,128)} async-done(((f32[1024,344]{1,0:T(8,128)}), f32[32,344]{1,0:T(8,128)}) %reduce-scatter.19.cloned.1.call-update) | async-done | bytes 44048 | tf_op jit(solution)/shard_map/reduce_scatter | solution.py:53
  637.4 117.7 %reduce-scatter.25.cloned.1.call-done = f32[64,128]{1,0:T(8,128)} async-done(((f32[2048,128]{1,0:T(8,128)}), f32[64,128]{1,0:T(8,128)}) %reduce-scatter.25.cloned.1.call-update) | async-done | bytes 32784
  (37 shorter events, 2.8 us)
Async XLA Ops:
  7.2 71.2 %copy-start = (bf16[1024,344]{0,1:T(8,128)(2,1)S(1)}, bf16[1024,344]{0,1:T(8,128)(2,1)}, u32[]{:S(2)}) copy-start(bf16[1024,344]{0,1:T(8,128)(2,1)} %param.9) | copy-start | bytes 2113540
  7.2 72.4 %copy-start.2 = (bf16[1024,344]{0,1:T(8,128)(2,1)S(1)}, bf16[1024,344]{0,1:T(8,128)(2,1)}, u32[]{:S(2)}) copy-start(bf16[1024,344]{0,1:T(8,128)(2,1)} %param.10) | copy-start | bytes 2113540
  7.2 126.0 %all-gather.3.cloned.1.call-start = ((), (), s32[]{:S(2)}) async-start(), calls=%async_computation.10 | async-start | bytes 1327104 | tf_op jit(solution)/shard_map/all_gather | solution.py:28
  79.5 150.9 %reduce-scatter.21.cloned.1.call-start = ((), (), s32[]{:S(2)}) async-start(), calls=%async_computation.11 | async-start | bytes 3170304
  139.0 3.9 copy-start.1
  139.0 3.9 copy-start.5
  142.9 1.4 copy-start.3
  147.7 169.4 %reduce-scatter.23.cloned.1.call-start = ((), (), s32[]{:S(2)}) async-start(), calls=%async_computation.12 | async-start | bytes 3170304
  153.4 243.8 %reduce-scatter.15.cloned.1.call-start = ((), (), s32[]{:S(2)}) async-start(), calls=%async_computation.7 | async-start | bytes 884736 | tf_op jit(solution)/shard_map/reduce_scatter | solution.py:56
  320.9 198.7 %reduce-scatter.17.cloned.1.call-start = ((), (), s32[]{:S(2)}) async-start(), calls=%async_computation.8 | async-start | bytes 1622016 | tf_op jit(solution)/shard_map/reduce_scatter | solution.py:52
  322.6 314.8 %reduce-scatter.19.cloned.1.call-start = ((), (), s32[]{:S(2)}) async-start(), calls=%async_computation.9 | async-start | bytes 1622016 | tf_op jit(solution)/shard_map/reduce_scatter | solution.py:53
  324.3 2.9 copy-start.6
  324.4 430.8 %reduce-scatter.25.cloned.1.call-start = ((), (), s32[]{:S(2)}) async-start(), calls=%async_computation.13 | async-start | bytes 1081344
  324.6 2.7 copy-start.4
  399.8 84.9 %copy-start.7 = (u32[256]{0:T(256)S(1)}, u32[256]{0:T(256)}, u32[]{:S(2)}) copy-start(u32[256]{0:T(256)} %constant.5) | copy-start | bytes 3076
  483.3 2.6 collective-permute-start
Sparse Core Ops, SparseCore 0:
  79.6 53.5 all-gather.2
  147.8 82.5 reduce-scatter.20
  234.5 82.5 reduce-scatter.22
  321.0 76.1 reduce-scatter.14
  400.1 119.4 reduce-scatter.16
  522.5 114.8 reduce-scatter.18
  640.5 114.6 reduce-scatter.24
